TPU v7x, 32 devices: a whole 2x2x4 slice. The times are simulated.
32 devices in a mesh: orow: 8 (over z, x), ocol: 4 (over y, core).
Axes of the slice: x: 2, y: 2, z: 4, core: 2. Of those that a mesh axis runs over, the one named last changes fastest.
Arguments:
- integrals: bfloat16 [2304, 16, 384], P('ocol', 'orow'), may hold values from -0.29882812 to 0.29882812
- occ_count: int32 [8], replicated, may hold values from 1 to 2
- occ_energy: float32 [16], replicated, may hold values from -2 to -0.5
- vir_energy: float32 [384], replicated, may hold values from 0.3 to 2.5
- task_iblock: int32 [32, 1], replicated, may hold values from 0 to 7; in each aligned block of 32 rows (0 to 31, 32 to 63, ...) at most 8 rows name the same one
- task_jblock: int32 [32], replicated, may hold values from 0 to 7
Outputs:
- gamma_out: float32 [2304, 16, 384], P('ocol', 'orow')
- density: float32 [384, 384], replicated
Inputs may be any that keep to these rules, and one draw needn't show every extreme that they name: `task_iblock`: no first block is named by more than 8 tasks, and some first block by exactly 8.
All inputs are finite; a program needn't handle non-finite values.
Results may differ from a plain program's by a relative error of at most 0.0019.
Values may be sent and summed in bfloat16 or wider, within the bound.
A program may use at most 128 MiB of HBM per device.

v0:
```python
import jax
import jax.numpy as jnp
from jax import lax
from jax.sharding import PartitionSpec as P


def make_amplitudes(k_total, i_energy, j_energy, vir_energy, usable):
    slots = k_total.shape[0]
    orbitals = i_energy.shape[1]
    virtuals = vir_energy.shape[0]
    k_grid = k_total.reshape(slots, orbitals, virtuals, orbitals, virtuals)
    denominator = (
        i_energy[:, :, None, None, None]
        + j_energy[:, None, None, :, None]
        - vir_energy[None, None, :, None, None]
        - vir_energy[None, None, None, None, :]
    )
    values = (2.0 * k_grid - jnp.swapaxes(k_grid, 2, 4)) / denominator
    values = values * usable[:, None, None, None, None]
    return values.astype(jnp.bfloat16).reshape(slots, orbitals * virtuals, orbitals * virtuals)


def local(integrals, occ_count, occ_energy, vir_energy, task_iblock, task_jblock):
    aux_local = integrals.shape[0]
    orbitals = integrals.shape[1]
    virtuals = integrals.shape[2]
    span = orbitals * virtuals
    block_total = lax.axis_size("orow")
    col_total = lax.axis_size("ocol")
    my_row = lax.axis_index("orow")
    my_col = lax.axis_index("ocol")
    active = jnp.arange(orbitals) < occ_count[my_row]
    masked = integrals * active.astype(jnp.bfloat16)[None, :, None]
    gathered = lax.all_gather(masked, "orow", axis=1, tiled=True)
    flat_blocks = gathered.reshape(aux_local, block_total, span)
    first_list = task_iblock[:, 0]
    task_total = first_list.shape[0]
    per_row = task_total // block_total
    task_ids = my_row * per_row + jnp.arange(per_row)
    i_block = first_list[task_ids]
    j_block = task_jblock[task_ids]
    usable = jnp.ones((per_row,), jnp.float32)
    energy_grid = occ_energy.reshape(block_total, orbitals)
    i_rows = jnp.take(flat_blocks, i_block, axis=1)
    j_rows = jnp.take(flat_blocks, j_block, axis=1)
    k_partial = jnp.einsum("psx,psy->sxy", i_rows, j_rows, preferred_element_type=jnp.float32)
    slots = k_partial.shape[0]
    i_energy = energy_grid[i_block]
    j_energy = energy_grid[j_block]
    k_total = lax.psum(k_partial, "ocol")
    amplitudes = make_amplitudes(k_total, i_energy, j_energy, vir_energy, usable)
    gamma_i = jnp.einsum("sxy,psy->psx", amplitudes, j_rows, preferred_element_type=jnp.float32)
    gamma_j = jnp.einsum("sxy,psx->psy", amplitudes, i_rows, preferred_element_type=jnp.float32)
    slice_width = span // col_total
    amp_grid = amplitudes.reshape(slots, orbitals, virtuals, span)
    column_part = lax.dynamic_slice_in_dim(amp_grid, my_col * slice_width, slice_width, 3)
    dens_part = jnp.einsum(
        "siaw,sibw->ab", column_part, column_part, preferred_element_type=jnp.float32
    )
    block_ids = jnp.arange(block_total)
    i_onehot = (i_block[:, None] == block_ids[None, :]).astype(jnp.float32)
    j_onehot = (j_block[:, None] == block_ids[None, :]).astype(jnp.float32)
    buffer = jnp.einsum(
        "sk,psx->pkx", i_onehot, gamma_i, precision=lax.Precision.HIGHEST
    ) + jnp.einsum("sk,psx->pkx", j_onehot, gamma_j, precision=lax.Precision.HIGHEST)
    owned = lax.psum_scatter(buffer, "orow", scatter_dimension=1, tiled=True)
    gamma_out = owned.reshape(aux_local, orbitals, virtuals)
    density = lax.psum(dens_part, ("orow", "ocol")) / task_total
    return (gamma_out, density)


def solution(mesh):
    return jax.shard_map(
        local,
        mesh=mesh,
        in_specs=(P("ocol", "orow", None), P(), P(), P(), P(), P()),
        out_specs=(P("ocol", "orow", None), P()),
        check_vma=False,
    )
```

profile of v0, /device:TPU:1, one launch (start us, length us, event | category | flops | bytes accessed | tf_op | source)
XLA Modules:
  0.0 801.1 jit_solution(11271543090973514411)
XLA Ops:
  7.2 0.0 copy-start
  7.2 0.0 all-gather.2.cloned.1.call-start
  7.2 1.2 dynamic_slice.6
  8.5 0.6 compare_convert_fusion
  9.1 2.3 copy_multiply_fusion
  11.4 0.0 all-gather.2.cloned.1.call-update
  11.4 0.0 all-reduce.3.cloned.1.call-start
  11.5 0.6 gather_fusion.1
  12.1 1.3 gather_fusion
  13.5 0.5 compare_and_fusion
  14.0 106.9 %all-gather.2.cloned.1.call-done = bf16[576,16,384]{2,0,1:T(8,128)(2,1)} async-done(((bf16[576,2,384]{2,0,1:T(8,128)(2,1)}), bf16[576,16,384]{2,0,1:T(8,128)(2,1)}) %all-gather.2.cloned.1.call-update) | async-done | bytes 7077904 | tf_op jit(solution)/shard_map/all_gather | solution.py:34
  120.9 10.1 %copy.40 = bf16[576,16,384]{2,1,0:T(8,128)(2,1)} copy(bf16[576,16,384]{2,0,1:T(8,128)(2,1)} %all-gather.2.cloned.1.call-done) | data formatting | bytes 14155776 | tf_op jit(solution)/shard_map/all_gather | solution.py:34
  131.0 11.3 %reshape.89 = bf16[576,8,768]{2,1,0:T(8,128)(2,1)} reshape(bf16[576,16,384]{2,1,0:T(8,128)(2,1)} %copy.40) | data formatting | bytes 14155776 | tf_op jit(solution)/shard_map/reshape | solution.py:35
  142.3 7.4 copy.41
  149.6 5.6 gather_fusion.5
  155.3 3.8 gather_fusion.4
  159.1 9.3 %fusion.7 = f32[4,768,768]{2,1,0:T(8,128)} fusion(bf16[4,576,768]{2,1,0:T(8,128)(2,1)S(1)} %gather_fusion.4, pred[4]{0:T(512)(128)(4,1)S(1)} %get-tuple-element.4, bf16[4,576,768]{2,1,0:T(8,128)(2,1)} %gather_fusion.5, pred[4]{0:T(512)(128)(4,1)S(1)} %copy-done.11), kind=kOutput, calls=%fused_computation.15 | convolution fusion | flops 2721447936 | bytes 16515080 | tf_op jit(solution)/shard_map/psx,psy->sxy/dot_general | solution.py:46
  168.4 12.5 %reshape.90 = f32[4,2,384,2,384]{4,3,2,1,0:T(2,128)} reshape(f32[4,768,768]{2,1,0:T(8,128)} %fusion.7) | data formatting | bytes 18874368 | tf_op jit(solution)/shard_map/reshape | solution.py:11
  180.9 14.8 %copy.43 = f32[4,2,384,2,384]{2,4,3,1,0:T(8,128)} copy(f32[4,2,384,2,384]{4,3,2,1,0:T(2,128)} %reshape.90) | data formatting | bytes 18874368 | tf_op jit(solution)/shard_map/reshape | solution.py:11
  195.7 0.0 all-reduce.3.cloned.1.call-update
  195.7 0.2 all-reduce.5.cloned.1.call-start
  195.9 0.4 copy-done.8
  196.3 0.1 reshape.91
  196.4 0.6 gather_fusion.3
  197.0 0.6 fusion.26
  197.6 0.6 pad_clamp_fusion.1
  198.2 0.7 gather_fusion.2
  198.9 0.1 broadcast_add_fusion
  199.0 0.7 broadcast_subtract_fusion
  199.6 165.0 %all-reduce.3.cloned.1.call-done = f32[4,2,384,2,384]{2,4,3,1,0:T(8,128)} async-done(((f32[4,2,384,2,384]{2,4,3,1,0:T(8,128)}), f32[4,2,384,2,384]{2,4,3,1,0:T(8,128)}) %all-reduce.3.cloned.1.call-update) | async-done | bytes 9437200 | tf_op jit(solution)/shard_map/psum | solution.py:50
  364.6 9.6 %copy.44 = f32[4,2,384,2,384]{4,2,3,1,0:T(8,128)} copy(f32[4,2,384,2,384]{2,4,3,1,0:T(8,128)} %all-reduce.3.cloned.1.call-done) | data formatting | bytes 18874368 | tf_op jit(solution)/shard_map/psum | solution.py:50
  374.2 9.6 %fusion.1 = bf16[4,2,384,2,384]{4,2,3,1,0:T(8,128)(2,1)} fusion(f32[4,2,384,2,384]{2,4,3,1,0:T(8,128)} %all-reduce.3.cloned.1.call-done, f32[4,2,384,2,384]{4,2,3,1,0:T(8,128)} %copy.44, f32[384]{0:T(512)S(1)} %copy-done.3, f32[4,2,384,2]{2,3,1,0:T(2,128)} %broadcast_subtract_fusion), kind=kLoop, calls=%fused_computation.9 | loop fusion | flops 11796480 | bytes 23619072 | tf_op jit(solution)/shard_map/convert_element_type | solution.py:20
  383.8 6.7 copy.52
  390.5 9.3 %copy.45 = bf16[4,2,384,2,384]{4,3,2,1,0:T(2,128)(2,1)} copy(bf16[4,2,384,2,384]{4,2,3,1,0:T(8,128)(2,1)} %fusion.1) | data formatting | bytes 9437184 | tf_op jit(solution)/shard_map/convert_element_type | solution.py:20
  399.8 11.3 %reshape.92 = bf16[4,768,768]{2,1,0:T(8,128)(2,1)} reshape(bf16[4,2,384,2,384]{4,3,2,1,0:T(2,128)(2,1)} %copy.45) | data formatting | bytes 9437184 | tf_op jit(solution)/shard_map/reshape | solution.py:20
  411.1 9.4 %fusion.15 = f32[576,4,768]{2,0,1:T(8,128)} fusion(bf16[4,768,768]{2,1,0:T(8,128)(2,1)} %reshape.92, bf16[4,576,768]{2,1,0:T(8,128)(2,1)} %gather_fusion.5, pred[4]{0:T(512)(128)(4,1)S(1)} %copy-done.12), kind=kOutput, calls=%fused_computation.23 | convolution fusion | flops 2719678464 | bytes 15335428 | tf_op jit(solution)/shard_map/sxy,psx->psy/dot_general | solution.py:53
  420.5 5.3 fusion.12
  425.8 3.3 convolution_bitcast_fusion
  429.1 0.0 all-reduce.5.cloned.1.call-update
  429.2 0.0 reduce-scatter.2.cloned.1.call-start
  429.2 14.4 %fusion.3 = f32[576,768,8]{1,2,0:T(8,128)S(1)} fusion(f32[576,4,768]{2,0,1:T(8,128)} %fusion.12, s32[4]{0:T(128)S(1)} %copy-done.5), kind=kOutput, calls=%fused_computation.11 | convolution fusion | flops 169869344 | bytes 21233680 | tf_op jit(solution)/shard_map/sk,psx->pkx/dot_general | solution.py:63
  443.7 18.4 %add_bitcast_fusion = f32[576,8,768]{2,1,0:T(8,128)} fusion(f32[576,768,8]{1,2,0:T(8,128)S(1)} %fusion.3, f32[576,4,768]{2,0,1:T(8,128)} %fusion.15, s32[4]{0:T(128)S(1)} %copy-done.7), kind=kOutput, calls=%fused_computation.6 | convolution fusion | flops 173408288 | bytes 35389456 | tf_op jit(solution)/shard_map/sk,psx->pkx/dot_general | solution.py:65
  462.1 14.7 %copy.48 = f32[576,8,768]{2,0,1:T(8,128)} copy(f32[576,8,768]{2,1,0:T(8,128)} %add_bitcast_fusion) | data formatting | bytes 28311552 | tf_op jit(solution)/shard_map/add | solution.py:63
  476.8 0.0 reduce-scatter.2.cloned.1.call-update
  476.8 81.5 %all-reduce.5.cloned.1.call-done = f32[384,384]{1,0:T(8,128)} async-done(((f32[384,384]{1,0:T(8,128)}), f32[384,384]{1,0:T(8,128)}) %all-reduce.5.cloned.1.call-update) | async-done | bytes 589840 | tf_op jit(solution)/shard_map/psum | solution.py:68
  558.3 1.9 broadcast_multiply_fusion
  560.2 230.8 %reduce-scatter.2.cloned.1.call-done = f32[576,1,768]{2,0,1:T(8,128)} async-done(((f32[576,8,768]{2,0,1:T(8,128)}), f32[576,1,768]{2,0,1:T(8,128)}) %reduce-scatter.2.cloned.1.call-update) | async-done | bytes 1769488 | tf_op jit(solution)/shard_map/reduce_scatter | solution.py:66
  791.0 3.1 reshape.93
  (32 shorter events, 0.1 us)
Async XLA Ops:
  7.2 4.3 copy-start
  7.2 113.7 %all-gather.2.cloned.1.call-start = ((), (), s32[]{:S(2)}) async-start(), calls=%async_computation.1 | async-start | bytes 7962624 | tf_op jit(solution)/shard_map/all_gather | solution.py:34
  11.4 353.2 %all-reduce.3.cloned.1.call-start = ((), (), s32[]{:S(2)}) async-start(), calls=%async_computation.2 | async-start | bytes 18874368 | tf_op jit(solution)/shard_map/psum | solution.py:50
  12.1 118.9 %copy-start.4 = (s32[4]{0:T(128)}, s32[4]{0:T(128)S(1)}, u32[]{:S(2)}) copy-start(s32[4]{0:T(128)S(1)} %gather_fusion.1) | copy-start | bytes 52
  13.4 183.0 %copy-start.6 = (s32[4]{0:T(128)}, s32[4]{0:T(128)S(1)}, u32[]{:S(2)}) copy-start(s32[4]{0:T(128)S(1)} %gather_fusion) | copy-start | bytes 52
  14.0 145.1 %copy-start.9 = (pred[4]{0:T(512)(128)(4,1)}, pred[4]{0:T(512)(128)(4,1)S(1)}, u32[]{:S(2)}) copy-start(pred[4]{0:T(512)(128)(4,1)S(1)} %get-tuple-element.4) | copy-start | bytes 16
  155.3 3.8 copy-start.11
  195.7 0.7 copy-start.8
  195.7 3.3 copy-start.3
  195.7 362.6 %all-reduce.5.cloned.1.call-start = ((), (), s32[]{:S(2)}) async-start(), calls=%async_computation.4 | async-start | bytes 1179648 | tf_op jit(solution)/shard_map/psum | solution.py:68
  399.8 11.4 %copy-start.12 = (pred[4]{0:T(512)(128)(4,1)S(1)}, pred[4]{0:T(512)(128)(4,1)}, u32[]{:S(2)}) copy-start(pred[4]{0:T(512)(128)(4,1)} %get-tuple-element.3) | copy-start | bytes 16
  411.1 9.4 %copy-start.2 = (bf16[4,768,768]{2,1,0:T(8,128)(2,1)S(1)}, bf16[4,768,768]{2,1,0:T(8,128)(2,1)}, u32[]{:S(2)}) copy-start(bf16[4,768,768]{2,1,0:T(8,128)(2,1)} %reshape.92) | copy-start | bytes 14155780
  411.1 9.4 %copy-start.10 = (pred[4]{0:T(512)(128)(4,1)S(1)}, pred[4]{0:T(512)(128)(4,1)}, u32[]{:S(2)}) copy-start(pred[4]{0:T(512)(128)(4,1)} %copy-done.9) | copy-start | bytes 16
  420.5 8.7 %copy-start.5 = (s32[4]{0:T(128)S(1)}, s32[4]{0:T(128)}, u32[]{:S(2)}) copy-start(s32[4]{0:T(128)} %copy-done.4) | copy-start | bytes 52
  429.2 14.5 %copy-start.7 = (s32[4]{0:T(128)S(1)}, s32[4]{0:T(128)}, u32[]{:S(2)}) copy-start(s32[4]{0:T(128)} %copy-done.6) | copy-start | bytes 52
  429.2 361.9 %reduce-scatter.2.cloned.1.call-start = ((), (), s32[]{:S(2)}) async-start(), calls=%async_computation.3 | async-start | bytes 15925248 | tf_op jit(solution)/shard_map/reduce_scatter | solution.py:66
  476.8 317.3 %copy-start.1 = (s32[32,1]{0,1:T(1,128)S(1)}, s32[32,1]{0,1:T(1,128)}, u32[]{:S(2)}) copy-start(s32[32,1]{0,1:T(1,128)} %param.12) | copy-start | bytes 388
Sparse Core Ops, SparseCore 0:
  11.5 109.2 all-gather.1
  195.8 168.7 all-reduce.2
  429.3 128.9 all-reduce.4
  561.8 229.1 reduce-scatter.1
where the time goes:
time: 811 us; the launch traced here: 801 us
  waiting for transfers between devices  584 us (72%)
  local copies, waits for them, and re-layouts  125 us (15%)
  matrix products  60.1 us (7%)
  other arithmetic  16.9 us (2%)
  between operations  14.4 us (2%)
    reduce_scatter x1, waiting for transfers between devices, local(): owned = lax.psum_scatter(buffer, 'orow', scatter_dimension=1, tiled=True)  231 us
    psum x1, waiting for transfers between devices, local(): k_total = lax.psum(k_partial, 'ocol')  165 us
    all_gather x1, waiting for transfers between devices, local(): gathered = lax.all_gather(masked, 'orow', axis=1, tiled=True)  107 us
    psum x1, waiting for transfers between devices, local(): density = lax.psum(dens_part, ('orow', 'ocol')) / task_total  81.5 us
    reshape x2, local copies, waits for them, and re-layouts, make_amplitudes(): k_grid = k_total.reshape(slots, orbitals, virtuals, orbitals, virtuals)  27.3 us
    reshape x2, local copies, waits for them, and re-layouts, local(): flat_blocks = gathered.reshape(aux_local, block_total, span)  18.6 us
    dot_general x1, matrix products, local(): jnp.einsum('sk,psx->pkx', j_onehot, gamma_j, precision=lax.Precision.HIGH...  18.4 us
  transfers between devices with their start and end apart: 4, of which 4 were waited for; matrix products, arithmetic and copies ran while one was open for 7% of the time, Pallas kernels for 0%

commit v1 on v0

v1 whole, which is shorter than its diff:
```python
import functools

import jax
import jax.numpy as jnp
from jax import lax
from jax.experimental import pallas as pl
from jax.experimental.pallas import tpu as pltpu
from jax.sharding import PartitionSpec as P


def pair_kernel(orbitals, cols, num_ref, occ_ref, gr_ref, gs_ref, gc_ref, vrow_ref, vcol_ref, gamma_ref, dens_ref, flip_ref):
    s = pl.program_id(0)
    blocks = pl.num_programs(0)
    row, col = num_ref[0], num_ref[1]
    virtuals = vrow_ref.shape[1]

    @pl.when(s == 0)
    def _():
        gamma_ref[...] = jnp.zeros_like(gamma_ref)
        dens_ref[...] = jnp.zeros_like(dens_ref)
        flip_ref[...] = gr_ref[0].T

    touch = num_ref[2 + s]
    first = num_ref[2 + blocks + s]

    @pl.when(touch > 0)
    def _():
        weight = touch.astype(jnp.float32)
        for i in range(orbitals):
            own = pl.ds(i * virtuals, virtuals)
            k_rows = jnp.dot(flip_ref[own, :], gs_ref[0], preferred_element_type=jnp.float32)
            parts = []
            for j in range(orbitals):
                k_ij = k_rows[:, j * virtuals:(j + 1) * virtuals]
                pair = occ_ref[row * orbitals + i] + occ_ref[s * orbitals + j]
                denominator = (pair - vcol_ref[...]) - vrow_ref[...]
                parts.append(((2.0 * k_ij - k_ij.T) / denominator).astype(jnp.bfloat16))
            amp = jnp.concatenate(parts, axis=1)
            gamma_ref[:, own] += weight * lax.dot_general(
                gc_ref[0], amp, (((1,), (1,)), ((), ())), preferred_element_type=jnp.float32)

            @pl.when((first > 0) & (lax.rem(s, cols) == col))
            def _():
                dens_ref[...] += first.astype(jnp.float32) * lax.dot_general(
                    amp, amp, (((1,), (1,)), ((), ())), preferred_element_type=jnp.float32)


def local(integrals, occ_count, occ_energy, vir_energy, task_iblock, task_jblock):
    aux_local, orbitals, virtuals = integrals.shape
    span = orbitals * virtuals
    blocks = lax.axis_size("orow")
    cols = lax.axis_size("ocol")
    row = lax.axis_index("orow")
    col = lax.axis_index("ocol")
    aux = aux_local * cols
    active = jnp.arange(orbitals) < occ_count[row]
    masked = integrals * active.astype(jnp.bfloat16)[None, :, None]
    shard = masked.reshape(aux_local, span)
    gathered = lax.all_gather(shard, ("orow", "ocol"), axis=0, tiled=True).reshape(blocks, aux, span)
    i_list, j_list = task_iblock[:, 0], task_jblock
    ids = jnp.arange(blocks)
    i_hot = i_list[None, :] == ids[:, None]
    j_hot = j_list[None, :] == ids[:, None]
    first = jnp.sum((i_list == row)[None, :] & j_hot, axis=1).astype(jnp.int32)
    second = jnp.sum((j_list == row)[None, :] & i_hot, axis=1).astype(jnp.int32)
    numbers = jnp.concatenate([jnp.stack([row, col]).astype(jnp.int32), first + second, first])
    gamma, dens = pl.pallas_call(
        functools.partial(pair_kernel, orbitals, cols),
        grid_spec=pltpu.PrefetchScalarGridSpec(
            num_scalar_prefetch=2,
            grid=(blocks,),
            in_specs=[
                pl.BlockSpec((1, aux, span), lambda s, num, occ: (num[0], 0, 0)),
                pl.BlockSpec((1, aux, span), lambda s, num, occ: (s, 0, 0)),
                pl.BlockSpec((1, aux_local, span), lambda s, num, occ: (s, num[1], 0)),
                pl.BlockSpec((1, virtuals), lambda s, num, occ: (0, 0)),
                pl.BlockSpec((virtuals, 1), lambda s, num, occ: (0, 0)),
            ],
            out_specs=[
                pl.BlockSpec((aux_local, span), lambda s, num, occ: (0, 0)),
                pl.BlockSpec((virtuals, virtuals), lambda s, num, occ: (0, 0)),
            ],
            scratch_shapes=[pltpu.VMEM((span, aux), jnp.bfloat16)],
        ),
        out_shape=[
            jax.ShapeDtypeStruct((aux_local, span), jnp.float32),
            jax.ShapeDtypeStruct((virtuals, virtuals), jnp.float32),
        ],
        compiler_params=pltpu.CompilerParams(vmem_limit_bytes=56 * 1024 * 1024),
    )(numbers, occ_energy, gathered, gathered, gathered, vir_energy[None, :], vir_energy[:, None])
    density = lax.psum(dens, ("orow", "ocol")) / i_list.shape[0]
    return gamma.reshape(aux_local, orbitals, virtuals), density


def solution(mesh):
    return jax.shard_map(
        local,
        mesh=mesh,
        in_specs=(P("ocol", "orow", None), P(), P(), P(), P(), P()),
        out_specs=(P("ocol", "orow", None), P()),
        check_vma=False,
    )
```

time: 811 us -> 369 us (0.45); the launches traced: 801 us -> 371 us
  waiting for transfers between devices: 584 us -> 302 us
  local copies, waits for them, and re-layouts: 125 us -> 6.73 us
  matrix products: 60.1 us -> 0 us
  Pallas kernels: 0 us -> 42.4 us
  other arithmetic: 16.9 us -> 5.48 us
    reduce_scatter x1 -> x0, waiting for transfers between devices: 231 us -> none  [local(): owned = lax.psum_scatter(buffer, 'orow', scatter_dimension=1, tiled=True)]
    psum x2 -> x1, waiting for transfers between devices: 246 us -> 133 us  [local(): density = lax.psum(dens, ('orow', 'ocol')) / i_list.shape[0]]
    all_gather x1, waiting for transfers between devices: 107 us -> 169 us  [local(): lax.all_gather(shard, ('orow', 'ocol'), axis=0, tiled=True)]
    dot_general x6 -> x0, matrix products: 60.1 us -> none  [the longest x1 18.4 us: local(): jnp.einsum('sk,psx->pkx', j_onehot, gamma_j, precision=lax.Precision.HIGH...]
    reshape x7 -> x1, local copies, waits for them, and re-layouts: 60.5 us -> 3.08 us  [local(): return (gamma.reshape(aux_local, orbitals, virtuals), density)]
    pallas_call x0 -> x1, Pallas kernels: none -> 42.4 us  [local(): pl.pallas_call(functools.partial(pair_kernel, orbitals, cols), grid_spec=...]
    add x1 -> x0, local copies, waits for them, and re-layouts: 14.7 us -> none  [local(): jnp.einsum('sk,psx->pkx', i_onehot, gamma_i, precision=lax.Precision.HIGH...]
    gather x6 -> x0, local copies, waits for them, and re-layouts: 12.6 us -> none  [the longest x1 5.61 us: local(): i_rows = jnp.take(flat_blocks, i_block, axis=1)]
  transfers between devices with their start and end apart: 4 -> 2, of which waited for: 4 -> 2; matrix products, arithmetic and copies ran while one was open for 7% -> 1% of each run, Pallas kernels for 0% -> 0%
where the time goes in v1:
time: 369 us; the launch traced here: 371 us
  waiting for transfers between devices  302 us (82%)
  Pallas kernels  42.4 us (11%)
  between operations  14.1 us (4%)
  local copies, waits for them, and re-layouts  6.73 us (2%)
  other arithmetic  5.48 us (1%)
    all_gather x1, waiting for transfers between devices, local(): lax.all_gather(shard, ('orow', 'ocol'), axis=0, tiled=True)  169 us
    psum x1, waiting for transfers between devices, local(): density = lax.psum(dens, ('orow', 'ocol')) / i_list.shape[0]  133 us
    pallas_call x1, Pallas kernels, local(): pl.pallas_call(functools.partial(pair_kernel, orbitals, cols), grid_spec=...  42.4 us
  transfers between devices with their start and end apart: 2, of which 2 were waited for; matrix products, arithmetic and copies ran while one was open for 1% of the time, Pallas kernels for 0%

profile of v1, /device:TPU:1, one launch (start us, length us, event | category | flops | bytes accessed | tf_op | source)
XLA Modules:
  0.0 370.8 jit_solution(5352919339585386605)
XLA Ops:
  7.2 0.0 all-gather.2.cloned.1.call-start
  7.2 1.2 dynamic_slice.3
  8.5 0.6 compare_convert_fusion
  9.1 2.0 broadcast_multiply_fusion
  11.1 0.0 copy-start
  11.1 0.0 copy-start.1
  11.1 0.0 copy-start.2
  11.1 1.1 copy.10
  12.2 0.0 all-gather.2.cloned.1.call-update
  12.2 0.0 all-reduce.2.cloned.1.call-start
  12.3 0.0 copy-done
  12.3 0.5 broadcast_in_dim.4.vrow_ref
  12.8 0.8 broadcast_in_dim.6.vcol_ref
  13.6 0.0 copy-done.1
  13.6 0.0 copy-done.2
  13.6 0.1 convert_reduce_fusion.1
  13.8 0.1 convert_reduce_fusion
  13.9 0.7 pad_add_fusion.num_ref
  14.6 169.4 %all-gather.2.cloned.1.call-done = bf16[18432,768]{1,0:T(8,128)(2,1)} async-done(((bf16[576,768]{1,0:T(8,128)(2,1)}), bf16[18432,768]{1,0:T(8,128)(2,1)}) %all-gather.2.cloned.1.call-update) | async-done | bytes 28311568 | tf_op jit(solution)/shard_map/all_gather | solution.py:59
  184.0 42.4 %shard_map.77 = (f32[576,768]{1,0:T(8,128)}, f32[384,384]{1,0:T(8,128)}) custom-call(s32[18]{0:T(128)} %pad_add_fusion.num_ref, f32[16]{0:T(128)} %occ_ref.1, bf16[8,2304,768]{2,1,0:T(8,128)(2,1)} %bitcast.8, bf16[8,2304,768]{2,1,0:T(8,128)(2,1)} %bitcast.9, bf16[8,2304,768]{2,1,0:T(8,128)(2,1)} %bitcast.10, f32[1,384]{1,0:T(1,128)} %broadcast_in_dim.4.vrow_ref, ...), custom_call_target="tpu_custom_call" | custom-call | tf_op jit(solution)/shard_map/pallas_call | solution.py:67
  226.4 0.0 all-reduce.2.cloned.1.call-update
  226.4 3.1 reshape.28
  229.5 132.5 %all-reduce.2.cloned.1.call-done = f32[384,384]{1,0:T(8,128)} async-done(((f32[384,384]{1,0:T(8,128)}), f32[384,384]{1,0:T(8,128)}) %all-reduce.2.cloned.1.call-update) | async-done | bytes 589840 | tf_op jit(solution)/shard_map/psum | solution.py:91
  362.0 1.9 broadcast_multiply_fusion.1
  (2 shorter events, 0.0 us)
Async XLA Ops:
  7.2 176.8 %all-gather.2.cloned.1.call-start = ((), (), s32[]{:S(2)}) async-start(), calls=%async_computation | async-start | bytes 29196288 | tf_op jit(solution)/shard_map/all_gather | solution.py:59
  11.1 1.2 copy-start
  11.1 2.5 copy-start.1
  11.1 2.5 copy-start.2
  12.2 349.8 %all-reduce.2.cloned.1.call-start = ((), (), s32[]{:S(2)}) async-start(), calls=%async_computation.1 | async-start | bytes 1179648 | tf_op jit(solution)/shard_map/psum | solution.py:91
Sparse Core Ops, SparseCore 0:
  12.3 171.5 all-gather.1
  226.5 135.4 all-reduce.1

commit v2 on v1

--- a/solution.py
+++ b/solution.py
@@ -7,8 +7,10 @@
 from jax.experimental.pallas import tpu as pltpu
 from jax.sharding import PartitionSpec as P
 
+MESH = pl.DeviceIdType.MESH
 
-def pair_kernel(orbitals, cols, num_ref, occ_ref, gr_ref, gs_ref, gc_ref, vrow_ref, vcol_ref, gamma_ref, dens_ref, flip_ref):
+
+def pair_kernel(orbitals, cols, num_ref, occ_ref, gr_ref, gs_ref, gc_ref, vrow_ref, vcol_ref, gamma_ref, dens_ref, flip_ref, amp_ref):
     s = pl.program_id(0)
     blocks = pl.num_programs(0)
     row, col = num_ref[0], num_ref[1]
@@ -36,13 +38,104 @@
                 denominator = (pair - vcol_ref[...]) - vrow_ref[...]
                 parts.append(((2.0 * k_ij - k_ij.T) / denominator).astype(jnp.bfloat16))
             amp = jnp.concatenate(parts, axis=1)
+            amp_ref[...] = amp
             gamma_ref[:, own] += weight * lax.dot_general(
                 gc_ref[0], amp, (((1,), (1,)), ((), ())), preferred_element_type=jnp.float32)
 
-            @pl.when((first > 0) & (lax.rem(s, cols) == col))
+            @pl.when(first > 0)
             def _():
+                strip = virtuals // cols
+                mine = amp_ref[pl.ds(pl.multiple_of(col * strip, strip), strip), :]
                 dens_ref[...] += first.astype(jnp.float32) * lax.dot_general(
-                    amp, amp, (((1,), (1,)), ((), ())), preferred_element_type=jnp.float32)
+                    mine, amp_ref[...], (((1,), (1,)), ((), ())), preferred_element_type=jnp.float32)
+
+
+def density_kernel(scale, part_ref, out_ref, arrived, send_sem, take_sem, pass_sem, row_sem, fan_sem, col_sem):
+    rows, cols = lax.axis_size("orow"), lax.axis_size("ocol")
+    row, col = lax.axis_index("orow"), lax.axis_index("ocol")
+    barrier = pltpu.get_barrier_semaphore()
+
+    def peer(step):
+        return lax.rem(row + step, rows)
+
+    def other(step):
+        return lax.rem(col + step, cols)
+
+    @pl.loop(1, rows)
+    def _(step):
+        pl.semaphore_signal(barrier, inc=1, device_id={"orow": peer(step)}, device_id_type=MESH)
+
+    @pl.loop(1, cols)
+    def _(step):
+        pl.semaphore_signal(barrier, inc=1, device_id={"ocol": other(step)}, device_id_type=MESH)
+
+    pl.semaphore_wait(barrier, rows + cols - 2)
+
+    def scatter(step):
+        return pltpu.make_async_remote_copy(
+            src_ref=part_ref.at[peer(step)], dst_ref=arrived.at[step - 1], send_sem=send_sem.at[step - 1],
+            recv_sem=take_sem.at[step - 1], device_id={"orow": peer(step)}, device_id_type=MESH)
+
+    def spread(step):
+        spot = out_ref.at[col, row]
+        return pltpu.make_async_remote_copy(
+            src_ref=spot, dst_ref=spot, send_sem=pass_sem.at[step - 1],
+            recv_sem=row_sem.at[step - 1], device_id={"orow": peer(step)}, device_id_type=MESH)
+
+    def fan(step):
+        spot = out_ref.at[col]
+        return pltpu.make_async_remote_copy(
+            src_ref=spot, dst_ref=spot, send_sem=fan_sem.at[step - 1],
+            recv_sem=col_sem.at[step - 1], device_id={"ocol": other(step)}, device_id_type=MESH)
+
+    @pl.loop(1, rows)
+    def _(step):
+        scatter(step).start()
+
+    total = part_ref[row]
+    for step in range(1, rows):
+        scatter(step).wait()
+        total = total + arrived[step - 1]
+    out_ref[col, row] = total * scale
+
+    @pl.loop(1, rows)
+    def _(step):
+        spread(step).start()
+
+    @pl.loop(1, rows)
+    def _(step):
+        spread(step).wait()
+
+    @pl.loop(1, cols)
+    def _(step):
+        fan(step).start()
+
+    @pl.loop(1, cols)
+    def _(step):
+        fan(step).wait()
+
+
+def sum_density(part, tasks):
+    rows, cols = lax.axis_size("orow"), lax.axis_size("ocol")
+    strip, virtuals = part.shape
+    share = strip // rows
+    full = pl.pallas_call(
+        functools.partial(density_kernel, 1.0 / tasks),
+        out_shape=jax.ShapeDtypeStruct((cols, rows, share, virtuals), jnp.float32),
+        in_specs=[pl.BlockSpec(memory_space=pltpu.VMEM)],
+        out_specs=pl.BlockSpec(memory_space=pltpu.VMEM),
+        scratch_shapes=[
+            pltpu.VMEM((rows - 1, share, virtuals), jnp.float32),
+            pltpu.SemaphoreType.DMA((rows - 1,)),
+            pltpu.SemaphoreType.DMA((rows - 1,)),
+            pltpu.SemaphoreType.DMA((rows - 1,)),
+            pltpu.SemaphoreType.DMA((rows - 1,)),
+            pltpu.SemaphoreType.DMA((cols - 1,)),
+            pltpu.SemaphoreType.DMA((cols - 1,)),
+        ],
+        compiler_params=pltpu.CompilerParams(collective_id=1, has_side_effects=True),
+    )(part.reshape(rows, share, virtuals))
+    return full.reshape(virtuals, virtuals)
 
 
 def local(integrals, occ_count, occ_energy, vir_energy, task_iblock, task_jblock):
@@ -78,17 +171,17 @@
             ],
             out_specs=[
                 pl.BlockSpec((aux_local, span), lambda s, num, occ: (0, 0)),
-                pl.BlockSpec((virtuals, virtuals), lambda s, num, occ: (0, 0)),
+                pl.BlockSpec((virtuals // cols, virtuals), lambda s, num, occ: (0, 0)),
             ],
-            scratch_shapes=[pltpu.VMEM((span, aux), jnp.bfloat16)],
+            scratch_shapes=[pltpu.VMEM((span, aux), jnp.bfloat16), pltpu.VMEM((virtuals, span), jnp.bfloat16)],
         ),
         out_shape=[
             jax.ShapeDtypeStruct((aux_local, span), jnp.float32),
-            jax.ShapeDtypeStruct((virtuals, virtuals), jnp.float32),
+            jax.ShapeDtypeStruct((virtuals // cols, virtuals), jnp.float32),
         ],
         compiler_params=pltpu.CompilerParams(vmem_limit_bytes=56 * 1024 * 1024),
     )(numbers, occ_energy, gathered, gathered, gathered, vir_energy[None, :], vir_energy[:, None])
-    density = lax.psum(dens, ("orow", "ocol")) / i_list.shape[0]
+    density = sum_density(dens, i_list.shape[0])
     return gamma.reshape(aux_local, orbitals, virtuals), density
 
 

time: 369 us -> 272 us (0.74)
  waiting for transfers between devices: 302 us -> 170 us
  Pallas kernels: 42.4 us -> 79.5 us
    psum x1 -> x0, waiting for transfers between devices: 133 us -> none  [local(): density = lax.psum(dens, ('orow', 'ocol')) / i_list.shape[0]]
    pallas_call x0 -> x1, Pallas kernels: none -> 32.7 us  [sum_density(): pl.pallas_call(functools.partial(density_kernel, 1.0 / tasks), out_shape=...]
    pallas_call x1, Pallas kernels: 42.4 us -> 46.7 us  [local(): pl.pallas_call(functools.partial(pair_kernel, orbitals, cols), grid_spec=...]
  transfers between devices with their start and end apart: 2 -> 1, of which waited for: 2 -> 1; matrix products, arithmetic and copies ran while one was open for 1% -> 1% of each run, Pallas kernels for 0% -> 0%
where the time goes in v2:
time: 272 us; the launch traced here: 276 us
  waiting for transfers between devices  170 us (62%)
  Pallas kernels  79.5 us (29%)
  between operations  14.1 us (5%)
  local copies, waits for them, and re-layouts  9.52 us (4%)
  other arithmetic  3.45 us (1%)
    all_gather x1, waiting for transfers between devices, local(): lax.all_gather(shard, ('orow', 'ocol'), axis=0, tiled=True)  170 us
    pallas_call x1, Pallas kernels, local(): pl.pallas_call(functools.partial(pair_kernel, orbitals, cols), grid_spec=...  46.7 us
    pallas_call x1, Pallas kernels, sum_density(): pl.pallas_call(functools.partial(density_kernel, 1.0 / tasks), out_shape=...  32.7 us
  transfers between devices with their start and end apart: 1, of which 1 were waited for; matrix products, arithmetic and copies ran while one was open for 1% of the time, Pallas kernels for 0%

profile of v2, /device:TPU:1, one launch (start us, length us, event | category | flops | bytes accessed | tf_op | source)
XLA Modules:
  0.0 276.1 jit_solution(12587652221217907245)
XLA Ops:
  7.2 0.0 all-gather.2.cloned.1.call-start
  7.2 1.2 dynamic_slice.3
  8.5 0.6 compare_convert_fusion
  9.1 2.0 broadcast_multiply_fusion
  11.1 0.0 copy-start.1
  11.1 0.0 copy-start.2
  11.1 0.0 copy-start.3
  11.1 1.1 copy.10
  12.2 0.0 all-gather.2.cloned.1.call-update
  12.2 0.0 copy-done.1
  12.2 0.6 broadcast_in_dim.4.vrow_ref
  12.8 0.8 broadcast_in_dim.6.vcol_ref
  13.6 0.0 copy-done.2
  13.6 0.0 copy-done.3
  13.6 0.1 convert_reduce_fusion.1
  13.8 0.1 convert_reduce_fusion
  13.9 0.6 pad_add_fusion.num_ref
  14.4 169.5 %all-gather.2.cloned.1.call-done = bf16[18432,768]{1,0:T(8,128)(2,1)} async-done(((bf16[576,768]{1,0:T(8,128)(2,1)}), bf16[18432,768]{1,0:T(8,128)(2,1)}) %all-gather.2.cloned.1.call-update) | async-done | bytes 28311568 | tf_op jit(solution)/shard_map/all_gather | solution.py:152
  184.0 46.7 %shard_map.77 = (f32[576,768]{1,0:T(8,128)}, f32[96,384]{1,0:T(8,128)}) custom-call(s32[18]{0:T(128)} %pad_add_fusion.num_ref, f32[16]{0:T(128)} %occ_ref.1, bf16[8,2304,768]{2,1,0:T(8,128)(2,1)} %bitcast.8, bf16[8,2304,768]{2,1,0:T(8,128)(2,1)} %bitcast.9, bf16[8,2304,768]{2,1,0:T(8,128)(2,1)} %bitcast.10, f32[1,384]{1,0:T(1,128)} %broadcast_in_dim.4.vrow_ref, ...), custom_call_target="tpu_custom_call" | custom-call | tf_op jit(solution)/shard_map/pallas_call | solution.py:160
  230.7 0.0 copy-start
  230.7 3.1 %reshape.34 = f32[576,2,384]{2,1,0:T(2,128)} reshape(f32[576,768]{1,0:T(8,128)} %get-tuple-element.4) | data formatting | bytes 3538944 | tf_op jit(solution)/shard_map/reshape | solution.py:185
  233.8 0.0 copy-done
  233.8 0.7 reshape.35.part_ref
  234.5 32.7 %shard_map.78 = f32[4,8,12,384]{3,2,1,0:T(8,128)} custom-call(f32[8,12,384]{2,1,0:T(8,128)} %reshape.35.part_ref), custom_call_target="tpu_custom_call" | custom-call | tf_op jit(solution)/shard_map/pallas_call | solution.py:122
  267.2 2.0 reshape.36
  (2 shorter events, 0.0 us)
Async XLA Ops:
  7.2 176.8 %all-gather.2.cloned.1.call-start = ((), (), s32[]{:S(2)}) async-start(), calls=%async_computation | async-start | bytes 29196288 | tf_op jit(solution)/shard_map/all_gather | solution.py:152
  11.1 1.1 copy-start.1
  11.1 2.5 copy-start.2
  11.1 2.5 copy-start.3
  230.7 3.1 %copy-start = (f32[96,384]{1,0:T(8,128)S(1)}, f32[96,384]{1,0:T(8,128)}, u32[]{:S(2)}) copy-start(f32[96,384]{1,0:T(8,128)} %get-tuple-element.5) | copy-start | bytes 442372
Sparse Core Ops, SparseCore 0:
  12.3 171.5 all-gather.1

commit v3 on v2

--- a/solution.py
+++ b/solution.py
@@ -138,6 +138,118 @@
     return full.reshape(virtuals, virtuals)
 
 
+def gather_kernel(nz, nx, ny, cut, shard_ref, all_ref, own_sem, send_sem, line_sem, pair_sem):
+    aux_local = shard_ref.shape[0]
+    row, col = lax.axis_index("orow"), lax.axis_index("ocol")
+    z, x, y, k = row // nx, lax.rem(row, nx), col // 2, lax.rem(col, 2)
+    spans = (pl.ds(0, cut), pl.ds(cut, aux_local - cut))
+
+    def turn(at, by, extent):
+        return lax.rem(at + by, extent)
+
+    def place(dz=0, dx=0, dy=0):
+        return turn(z, dz, nz) * nx + turn(x, dx, nx), turn(y, dy, ny)
+
+    def device(dz=0, dx=0, dy=0, dk=0):
+        r, c = place(dz, dx, dy)
+        return {"orow": r, "ocol": c * 2 + lax.rem(k + dk, 2)}
+
+    near = sorted(range(1, nz), key=lambda d: min(d, nz - d))
+    lines = {
+        "z": [dict(dz=d) for d in near],
+        "x": [dict(dx=d) for d in range(1, nx)],
+        "y": [dict(dy=d) for d in range(1, ny)],
+    }
+    peers = lines["z"] + lines["x"] + lines["y"] + [dict(dk=1)]
+    barrier = pltpu.get_barrier_semaphore()
+    for peer in peers:
+        pl.semaphore_signal(barrier, inc=1, device_id=device(**peer), device_id_type=MESH)
+    pl.semaphore_wait(barrier, len(peers))
+
+    sent = []
+
+    def push(piece, at, source, sem, peer):
+        r, c = place(**at)
+        copy = pltpu.make_async_remote_copy(
+            src_ref=source, dst_ref=all_ref.at[r, c * 2 + k, spans[piece]], send_sem=send_sem.at[len(sent)],
+            recv_sem=sem, device_id=device(**peer), device_id_type=MESH)
+        copy.start()
+        sent.append(copy)
+
+    def pass_on(piece, at, order):
+        r, c = place(**at)
+        own = not at
+        source = shard_ref.at[spans[piece]] if own else all_ref.at[r, c * 2 + k, spans[piece]]
+        for axis in order:
+            for peer in lines[axis]:
+                push(piece, at, source, line_sem.at[piece, r, c], peer)
+        push(piece, at, source, pair_sem.at[piece, r, c], dict(dk=1))
+
+    def take(piece, at, sem, core):
+        r, c = place(**at)
+        spot = all_ref.at[r, c * 2 + core, spans[piece]]
+        pltpu.make_async_remote_copy(
+            src_ref=spot, dst_ref=spot, send_sem=send_sem.at[0], recv_sem=sem.at[piece, r, c],
+            device_id=device(dk=1), device_id_type=MESH).wait_recv()
+
+    def relay(piece, at, order):
+        take(piece, at, line_sem, k)
+        pass_on(piece, at, order)
+
+    keep = pltpu.make_async_copy(shard_ref, all_ref.at[row, col], own_sem)
+    keep.start()
+    pass_on(1, {}, "yzx")
+    pass_on(0, {}, "zxy")
+    for side in lines["y"]:
+        relay(1, side, "zx")
+    for up in lines["z"]:
+        relay(0, up, "xy")
+    for up in [{}] + lines["z"]:
+        for across in lines["x"]:
+            relay(0, up | across, "y")
+        if up:
+            for side in [{}] + lines["y"]:
+                relay(1, up | side, "x")
+    for up in [{}] + lines["z"]:
+        for across in [{}] + lines["x"]:
+            for side in lines["y"]:
+                relay(0, up | across | side, "")
+        for side in [{}] + lines["y"]:
+            for across in lines["x"]:
+                relay(1, up | across | side, "")
+    for dz in range(nz):
+        for dx in range(nx):
+            for dy in range(ny):
+                for piece in (0, 1):
+                    take(piece, dict(dz=dz, dx=dx, dy=dy), pair_sem, 1 - k)
+    keep.wait()
+    for copy in sent:
+        copy.wait_send()
+
+
+def gather_all(shard):
+    rows, cols = lax.axis_size("orow"), lax.axis_size("ocol")
+    ny = cols // 2
+    nx = ny if rows % ny == 0 else 1
+    nz = rows // nx
+    aux_local, span = shard.shape
+    cut = aux_local * 5 // 9 // 16 * 16
+    pushes = 2 * nz * nx * ny + (nz - 1) + nz * (nx - 1) + nz * nx * (ny - 1) + (ny - 1) + ny * (nz - 1) + nz * ny * (nx - 1)
+    return pl.pallas_call(
+        functools.partial(gather_kernel, nz, nx, ny, cut),
+        out_shape=jax.ShapeDtypeStruct((rows, cols, aux_local, span), shard.dtype),
+        in_specs=[pl.BlockSpec(memory_space=pltpu.VMEM)],
+        out_specs=pl.BlockSpec(memory_space=pl.ANY),
+        scratch_shapes=[
+            pltpu.SemaphoreType.DMA,
+            pltpu.SemaphoreType.DMA((pushes,)),
+            pltpu.SemaphoreType.DMA((2, rows, ny)),
+            pltpu.SemaphoreType.DMA((2, rows, ny)),
+        ],
+        compiler_params=pltpu.CompilerParams(collective_id=2, has_side_effects=True),
+    )(shard)
+
+
 def local(integrals, occ_count, occ_energy, vir_energy, task_iblock, task_jblock):
     aux_local, orbitals, virtuals = integrals.shape
     span = orbitals * virtuals
@@ -149,7 +261,7 @@
     active = jnp.arange(orbitals) < occ_count[row]
     masked = integrals * active.astype(jnp.bfloat16)[None, :, None]
     shard = masked.reshape(aux_local, span)
-    gathered = lax.all_gather(shard, ("orow", "ocol"), axis=0, tiled=True).reshape(blocks, aux, span)
+    gathered = gather_all(shard).reshape(blocks, aux, span)
     i_list, j_list = task_iblock[:, 0], task_jblock
     ids = jnp.arange(blocks)
     i_hot = i_list[None, :] == ids[:, None]

time: 272 us -> 256 us (0.941); the launches traced: 276 us -> 252 us
  waiting for transfers between devices: 170 us -> 0 us
  Pallas kernels: 79.5 us -> 235 us
  between operations: 14.1 us -> 0.67 us
    all_gather x1 -> x0, waiting for transfers between devices: 170 us -> none  [local(): lax.all_gather(shard, ('orow', 'ocol'), axis=0, tiled=True)]
    pallas_call x0 -> x1, Pallas kernels: none -> 166 us  [gather_all(): pl.pallas_call(functools.partial(gather_kernel, nz, nx, ny, cut), out_sha...]
    pallas_call x1, Pallas kernels: 46.7 us -> 37.2 us  [local(): pl.pallas_call(functools.partial(pair_kernel, orbitals, cols), grid_spec=...]
  transfers between devices with their start and end apart: 1 -> 0, of which waited for: 1 -> 0; matrix products, arithmetic and copies ran while one was open for 1% -> 0% of each run, Pallas kernels for 0% -> 0%
where the time goes in v3:
time: 256 us; the launch traced here: 252 us
  Pallas kernels  235 us (92%)
  local copies, waits for them, and re-layouts  10.9 us (4%)
  other arithmetic  5.49 us (2%)
    pallas_call x1, Pallas kernels, gather_all(): pl.pallas_call(functools.partial(gather_kernel, nz, nx, ny, cut), out_sha...  166 us
    pallas_call x1, Pallas kernels, local(): pl.pallas_call(functools.partial(pair_kernel, orbitals, cols), grid_spec=...  37.2 us
    pallas_call x1, Pallas kernels, sum_density(): pl.pallas_call(functools.partial(density_kernel, 1.0 / tasks), out_shape=...  31.8 us

profile of v3, /device:TPU:1, one launch (start us, length us, event | category | flops | bytes accessed | tf_op | source)
XLA Modules:
  0.0 251.7 jit_solution(17454573836021803480)
XLA Ops:
  0.6 1.3 dynamic_slice.3
  2.0 0.7 compare_convert_fusion
  2.7 0.7 broadcast_compare_fusion
  3.3 0.8 convert_reduce_fusion
  4.1 0.8 convert_reduce_fusion.1
  4.9 0.6 pad_add_fusion.num_ref
  5.5 1.3 broadcast_in_dim.4.vrow_ref
  6.7 1.5 broadcast_in_dim.6.vcol_ref
  8.2 2.0 broadcast_multiply_fusion
  10.2 1.1 copy.10
  11.3 165.7 %shard_map.77 = bf16[8,4,576,768]{3,2,1,0:T(8,128)(2,1)} custom-call(bf16[576,768]{1,0:T(8,128)(2,1)} %bitcast.12), custom_call_target="tpu_custom_call" | custom-call | tf_op jit(solution)/shard_map/pallas_call | solution.py:238
  176.9 37.2 %shard_map.78 = (f32[576,768]{1,0:T(8,128)}, f32[96,384]{1,0:T(8,128)}) custom-call(s32[18]{0:T(128)} %pad_add_fusion.num_ref, f32[16]{0:T(128)} %occ_ref.1, bf16[8,2304,768]{2,1,0:T(8,128)(2,1)} %bitcast.8, bf16[8,2304,768]{2,1,0:T(8,128)(2,1)} %bitcast.9, bf16[8,2304,768]{2,1,0:T(8,128)(2,1)} %bitcast.10, f32[1,384]{1,0:T(1,128)} %broadcast_in_dim.4.vrow_ref, ...), custom_call_target="tpu_custom_call" | custom-call | tf_op jit(solution)/shard_map/pallas_call | solution.py:272
  214.1 0.0 copy-start
  214.1 3.1 %reshape.34 = f32[576,2,384]{2,1,0:T(2,128)} reshape(f32[576,768]{1,0:T(8,128)} %get-tuple-element.4) | data formatting | bytes 3538944 | tf_op jit(solution)/shard_map/reshape | solution.py:297
  217.2 0.0 copy-done
  217.2 0.7 reshape.35.part_ref
  217.9 31.8 %shard_map.79 = f32[4,8,12,384]{3,2,1,0:T(8,128)} custom-call(f32[8,12,384]{2,1,0:T(8,128)} %reshape.35.part_ref), custom_call_target="tpu_custom_call" | custom-call | tf_op jit(solution)/shard_map/pallas_call | solution.py:122
  249.7 2.0 reshape.36
  (1 shorter events, 0.0 us)
Async XLA Ops:
  214.1 3.1 %copy-start = (f32[96,384]{1,0:T(8,128)S(1)}, f32[96,384]{1,0:T(8,128)}, u32[]{:S(2)}) copy-start(f32[96,384]{1,0:T(8,128)} %get-tuple-element.5) | copy-start | bytes 442372

commit v4 on v3

--- a/solution.py
+++ b/solution.py
@@ -38,16 +38,18 @@
                 denominator = (pair - vcol_ref[...]) - vrow_ref[...]
                 parts.append(((2.0 * k_ij - k_ij.T) / denominator).astype(jnp.bfloat16))
             amp = jnp.concatenate(parts, axis=1)
-            amp_ref[...] = amp
+            amp_ref[i] = amp
             gamma_ref[:, own] += weight * lax.dot_general(
                 gc_ref[0], amp, (((1,), (1,)), ((), ())), preferred_element_type=jnp.float32)
 
-            @pl.when(first > 0)
-            def _():
-                strip = virtuals // cols
-                mine = amp_ref[pl.ds(pl.multiple_of(col * strip, strip), strip), :]
-                dens_ref[...] += first.astype(jnp.float32) * lax.dot_general(
-                    mine, amp_ref[...], (((1,), (1,)), ((), ())), preferred_element_type=jnp.float32)
+        @pl.when(first > 0)
+        def _():
+            strip = virtuals // cols
+            count = first.astype(jnp.float32)
+            for i in range(orbitals):
+                mine = amp_ref[i, pl.ds(pl.multiple_of(col * strip, strip), strip), :]
+                dens_ref[...] += count * lax.dot_general(
+                    mine, amp_ref[i], (((1,), (1,)), ((), ())), preferred_element_type=jnp.float32)
 
 
 def density_kernel(scale, part_ref, out_ref, arrived, send_sem, take_sem, pass_sem, row_sem, fan_sem, col_sem):
@@ -233,7 +235,7 @@
     nx = ny if rows % ny == 0 else 1
     nz = rows // nx
     aux_local, span = shard.shape
-    cut = aux_local * 5 // 9 // 16 * 16
+    cut = aux_local * 7 // 11 // 16 * 16
     pushes = 2 * nz * nx * ny + (nz - 1) + nz * (nx - 1) + nz * nx * (ny - 1) + (ny - 1) + ny * (nz - 1) + nz * ny * (nx - 1)
     return pl.pallas_call(
         functools.partial(gather_kernel, nz, nx, ny, cut),
@@ -285,7 +287,7 @@
                 pl.BlockSpec((aux_local, span), lambda s, num, occ: (0, 0)),
                 pl.BlockSpec((virtuals // cols, virtuals), lambda s, num, occ: (0, 0)),
             ],
-            scratch_shapes=[pltpu.VMEM((span, aux), jnp.bfloat16), pltpu.VMEM((virtuals, span), jnp.bfloat16)],
+            scratch_shapes=[pltpu.VMEM((span, aux), jnp.bfloat16), pltpu.VMEM((orbitals, virtuals, span), jnp.bfloat16)],
         ),
         out_shape=[
             jax.ShapeDtypeStruct((aux_local, span), jnp.float32),

time: 256 us -> 245 us (0.957)
  Pallas kernels: 235 us -> 226 us
    pallas_call x1, Pallas kernels: 31.8 us -> 26.5 us  [sum_density(): pl.pallas_call(functools.partial(density_kernel, 1.0 / tasks), out_shape=...]
    pallas_call x1, Pallas kernels: 166 us -> 162 us  [gather_all(): pl.pallas_call(functools.partial(gather_kernel, nz, nx, ny, cut), out_sha...]
where the time goes in v4:
time: 245 us; the launch traced here: 243 us
  Pallas kernels  226 us (92%)
  local copies, waits for them, and re-layouts  10.9 us (4%)
  other arithmetic  5.49 us (2%)
    pallas_call x1, Pallas kernels, gather_all(): pl.pallas_call(functools.partial(gather_kernel, nz, nx, ny, cut), out_sha...  162 us
    pallas_call x1, Pallas kernels, local(): pl.pallas_call(functools.partial(pair_kernel, orbitals, cols), grid_spec=...  37.9 us
    pallas_call x1, Pallas kernels, sum_density(): pl.pallas_call(functools.partial(density_kernel, 1.0 / tasks), out_shape=...  26.5 us

profile of v4, /device:TPU:1, one launch (start us, length us, event | category | flops | bytes accessed | tf_op | source)
XLA Modules:
  0.0 243.2 jit_solution(3499566605245014984)
XLA Ops:
  0.6 1.3 dynamic_slice.3
  2.0 0.7 compare_convert_fusion
  2.7 0.7 broadcast_compare_fusion
  3.3 0.8 convert_reduce_fusion
  4.1 0.8 convert_reduce_fusion.1
  4.9 0.6 pad_add_fusion.num_ref
  5.5 1.3 broadcast_in_dim.4.vrow_ref
  6.7 1.5 broadcast_in_dim.6.vcol_ref
  8.2 2.0 broadcast_multiply_fusion
  10.2 1.1 copy.10
  11.3 161.7 %shard_map.77 = bf16[8,4,576,768]{3,2,1,0:T(8,128)(2,1)} custom-call(bf16[576,768]{1,0:T(8,128)(2,1)} %bitcast.12), custom_call_target="tpu_custom_call" | custom-call | tf_op jit(solution)/shard_map/pallas_call | solution.py:240
  173.0 37.9 %shard_map.78 = (f32[576,768]{1,0:T(8,128)}, f32[96,384]{1,0:T(8,128)}) custom-call(s32[18]{0:T(128)} %pad_add_fusion.num_ref, f32[16]{0:T(128)} %occ_ref.1, bf16[8,2304,768]{2,1,0:T(8,128)(2,1)} %bitcast.8, bf16[8,2304,768]{2,1,0:T(8,128)(2,1)} %bitcast.9, bf16[8,2304,768]{2,1,0:T(8,128)(2,1)} %bitcast.10, f32[1,384]{1,0:T(1,128)} %broadcast_in_dim.4.vrow_ref, ...), custom_call_target="tpu_custom_call" | custom-call | tf_op jit(solution)/shard_map/pallas_call | solution.py:274
  210.9 0.0 copy-start
  210.9 3.1 %reshape.34 = f32[576,2,384]{2,1,0:T(2,128)} reshape(f32[576,768]{1,0:T(8,128)} %get-tuple-element.4) | data formatting | bytes 3538944 | tf_op jit(solution)/shard_map/reshape | solution.py:299
  214.0 0.0 copy-done
  214.0 0.7 reshape.35.part_ref
  214.7 26.5 %shard_map.79 = f32[4,8,12,384]{3,2,1,0:T(8,128)} custom-call(f32[8,12,384]{2,1,0:T(8,128)} %reshape.35.part_ref), custom_call_target="tpu_custom_call" | custom-call | tf_op jit(solution)/shard_map/pallas_call | solution.py:124
  241.2 2.0 reshape.36
  (1 shorter events, 0.0 us)
Async XLA Ops:
  210.9 3.1 %copy-start = (f32[96,384]{1,0:T(8,128)S(1)}, f32[96,384]{1,0:T(8,128)}, u32[]{:S(2)}) copy-start(f32[96,384]{1,0:T(8,128)} %get-tuple-element.5) | copy-start | bytes 442372

commit v5 on v4

--- a/solution.py
+++ b/solution.py
@@ -235,7 +235,7 @@
     nx = ny if rows % ny == 0 else 1
     nz = rows // nx
     aux_local, span = shard.shape
-    cut = aux_local * 7 // 11 // 16 * 16
+    cut = aux_local * 2 // 3 // 16 * 16
     pushes = 2 * nz * nx * ny + (nz - 1) + nz * (nx - 1) + nz * nx * (ny - 1) + (ny - 1) + ny * (nz - 1) + nz * ny * (nx - 1)
     return pl.pallas_call(
         functools.partial(gather_kernel, nz, nx, ny, cut),

time: 245 us -> 255 us (1.041)
  Pallas kernels: 226 us -> 237 us
    pallas_call x1, Pallas kernels: 37.9 us -> 41.8 us  [local(): pl.pallas_call(functools.partial(pair_kernel, orbitals, cols), grid_spec=...]
    pallas_call x1, Pallas kernels: 26.5 us -> 30.1 us  [sum_density(): pl.pallas_call(functools.partial(density_kernel, 1.0 / tasks), out_shape=...]
    pallas_call x1, Pallas kernels: 162 us -> 165 us  [gather_all(): pl.pallas_call(functools.partial(gather_kernel, nz, nx, ny, cut), out_sha...]
where the time goes in v5:
time: 255 us; the launch traced here: 254 us
  Pallas kernels  237 us (93%)
  local copies, waits for them, and re-layouts  10.9 us (4%)
  other arithmetic  5.49 us (2%)
    pallas_call x1, Pallas kernels, gather_all(): pl.pallas_call(functools.partial(gather_kernel, nz, nx, ny, cut), out_sha...  165 us
    pallas_call x1, Pallas kernels, local(): pl.pallas_call(functools.partial(pair_kernel, orbitals, cols), grid_spec=...  41.8 us
    pallas_call x1, Pallas kernels, sum_density(): pl.pallas_call(functools.partial(density_kernel, 1.0 / tasks), out_shape=...  30.1 us

profile of v5, /device:TPU:1, one launch (start us, length us, event | category | flops | bytes accessed | tf_op | source)
XLA Modules:
  0.0 253.7 jit_solution(13595472099532797268)
XLA Ops:
  0.6 1.3 dynamic_slice.3
  2.0 0.7 compare_convert_fusion
  2.7 0.7 broadcast_compare_fusion
  3.3 0.8 convert_reduce_fusion
  4.1 0.8 convert_reduce_fusion.1
  4.9 0.6 pad_add_fusion.num_ref
  5.5 1.3 broadcast_in_dim.4.vrow_ref
  6.7 1.5 broadcast_in_dim.6.vcol_ref
  8.2 2.0 broadcast_multiply_fusion
  10.2 1.1 copy.10
  11.3 164.8 %shard_map.77 = bf16[8,4,576,768]{3,2,1,0:T(8,128)(2,1)} custom-call(bf16[576,768]{1,0:T(8,128)(2,1)} %bitcast.12), custom_call_target="tpu_custom_call" | custom-call | tf_op jit(solution)/shard_map/pallas_call | solution.py:240
  176.0 41.8 %shard_map.78 = (f32[576,768]{1,0:T(8,128)}, f32[96,384]{1,0:T(8,128)}) custom-call(s32[18]{0:T(128)} %pad_add_fusion.num_ref, f32[16]{0:T(128)} %occ_ref.1, bf16[8,2304,768]{2,1,0:T(8,128)(2,1)} %bitcast.8, bf16[8,2304,768]{2,1,0:T(8,128)(2,1)} %bitcast.9, bf16[8,2304,768]{2,1,0:T(8,128)(2,1)} %bitcast.10, f32[1,384]{1,0:T(1,128)} %broadcast_in_dim.4.vrow_ref, ...), custom_call_target="tpu_custom_call" | custom-call | tf_op jit(solution)/shard_map/pallas_call | solution.py:274
  217.8 0.0 copy-start
  217.8 3.1 %reshape.34 = f32[576,2,384]{2,1,0:T(2,128)} reshape(f32[576,768]{1,0:T(8,128)} %get-tuple-element.4) | data formatting | bytes 3538944 | tf_op jit(solution)/shard_map/reshape | solution.py:299
  220.9 0.0 copy-done
  220.9 0.7 reshape.35.part_ref
  221.6 30.1 %shard_map.79 = f32[4,8,12,384]{3,2,1,0:T(8,128)} custom-call(f32[8,12,384]{2,1,0:T(8,128)} %reshape.35.part_ref), custom_call_target="tpu_custom_call" | custom-call | tf_op jit(solution)/shard_map/pallas_call | solution.py:124
  251.7 2.0 reshape.36
  (1 shorter events, 0.0 us)
Async XLA Ops:
  217.8 3.1 %copy-start = (f32[96,384]{1,0:T(8,128)S(1)}, f32[96,384]{1,0:T(8,128)}, u32[]{:S(2)}) copy-start(f32[96,384]{1,0:T(8,128)} %get-tuple-element.5) | copy-start | bytes 442372
